TPU v7x, 512 devices: a whole 4x4x16 slice. The times are simulated.
512 devices in a mesh: cell: 64 (over z, y), help: 8 (over x, core).
Axes of the slice: x: 4, y: 4, z: 16, core: 2. Of those that a mesh axis runs over, the one named last changes fastest.
Arguments:
- weights: float32 [64, 896, 896], P('cell', 'help'), may hold values from 1 to 4096
- counts: int32 [64], P('cell'), may hold values from 224 to 896, as said below
- select: int32 [64, 128], P('cell'), may hold values from 0 to 895, as said below
- cut_weights: bfloat16 [64, 128, 8192], P('cell', 'help'), may hold values from 1 to 256
Outputs:
- parent_rows: float32 [64, 128, 8192], P('cell', 'help')
Inputs may be any that keep to these rules, and one draw needn't show every extreme that they name: `counts`: one cell's count is exactly 896. `select`: each row holds 128 distinct vertex numbers of its cell, each below that cell's count.
All inputs are finite; a program needn't handle non-finite values.
Results may differ from a plain program's by a relative error of at most 0.0003.
Values sent between devices are 32-bit elements; how exact they have to be, the bound alone decides.
A program may use at most 64 MiB of HBM per device.

v0:
```python
import jax
import jax.numpy as jnp
from jax import lax
from jax.sharding import PartitionSpec as P

SQUARINGS = 2


LIMIT = 1048576.0
SCALE = 0.00390625


def largest_divisor(amount, ceiling):
    result = 1
    while result * 2 <= ceiling and amount % (result * 2) == 0:
        result = result * 2
    return result


def relax_pair(running, portion, current):
    amount = portion.shape[1]
    blocks = largest_divisor(amount, 16)

    def relax_one_block(block_index, current_best):
        first_index = block_index * blocks
        left_terms = lax.dynamic_slice_in_dim(current, first_index, blocks, 2)
        right_terms = lax.dynamic_slice_in_dim(portion, first_index, blocks, 1)
        return jnp.minimum(
            current_best, jnp.min(left_terms[:, :, :, None] + right_terms[:, None, :, :], axis=2)
        )

    return lax.fori_loop(0, amount // blocks, relax_one_block, running)


def per_device(weights, counts, select, cut_weights):
    groups, rows_here, capacity = weights.shape
    helpers = lax.axis_size("help")
    helper = lax.axis_index("help")
    first_row = helper * rows_here
    row_ids = first_row + lax.broadcasted_iota(jnp.int32, weights.shape, 1)
    col_ids = lax.broadcasted_iota(jnp.int32, weights.shape, 2)
    limits = counts[:, None, None]
    usable = (row_ids < limits) & (col_ids < limits)
    current = jnp.where(row_ids == col_ids, 0.0, jnp.where(usable, weights, LIMIT))
    for round_number in range(SQUARINGS):

        def fold_rows(running, portion, offset, current=current):
            return relax_pair(running, portion, current)

        current = fold_rows(
            jnp.full(current.shape, LIMIT, jnp.float32),
            lax.all_gather(current, "help", axis=1, tiled=True),
            jnp.int32(0),
        )
    width_pick = select.shape[1]
    expanded = jnp.broadcast_to(select[:, None, :], (groups, rows_here, width_pick))
    picked = jnp.take_along_axis(current, expanded, axis=2)
    position = select - first_row
    inside = (position >= 0) & (position < rows_here)
    clipped = jnp.clip(position, 0, rows_here - 1)
    row_index = jnp.broadcast_to(clipped[:, :, None], (groups, width_pick, width_pick))
    gathered = jnp.take_along_axis(picked, row_index, axis=1)
    placed = jnp.where(inside[:, :, None], gathered, 0.0)
    share = width_pick // helpers
    cells_total = cut_weights.shape[2] // width_pick
    row_count = groups * share
    initial = jnp.full((row_count, cells_total, width_pick), LIMIT, jnp.float32)
    own_rows = lax.psum_scatter(placed, "help", scatter_dimension=1, tiled=True)
    portion = lax.all_gather(own_rows, ("cell", "help"), axis=0, tiled=True)
    piece_rows = width_pick // helpers
    cut_view = cut_weights.reshape(row_count, cells_total * helpers, piece_rows)
    amount = portion.shape[0]
    blocks = largest_divisor(amount, max(1, 512 // piece_rows))

    def make_one_block(block_index, current_best):
        unit_ids = block_index * blocks + lax.iota(jnp.int32, blocks)
        owners = unit_ids // groups // helpers * groups + unit_ids % groups
        columns = owners * helpers + unit_ids // groups % helpers
        left_terms = jnp.take(cut_view, columns, axis=1).astype(jnp.float32)
        right_terms = lax.dynamic_slice_in_dim(portion, block_index * blocks, blocks, 0)
        best_paths = jnp.min(left_terms[:, :, :, None] + right_terms[None, :, :, :], axis=2)
        return current_best.at[:, owners, :].min(best_paths)

    running = lax.fori_loop(0, amount // blocks, make_one_block, initial)
    parent_view = running.reshape(groups, share, cells_total, width_pick)
    own_ids = lax.axis_index("cell") * groups + lax.iota(jnp.int32, groups)
    child_ids = lax.iota(jnp.int32, cells_total)
    mine = child_ids[None, :] == own_ids[:, None]
    merged = jnp.where(
        mine[:, None, :, None], jnp.minimum(parent_view, own_rows[:, :, None, :]), parent_view
    )
    return merged.reshape(groups, share, cells_total * width_pick) * SCALE


def solution(mesh):
    in_specs = (P("cell", "help", None), P("cell"), P("cell", None), P("cell", "help", None))
    out_specs = P("cell", "help", None)
    return jax.shard_map(
        per_device, mesh=mesh, in_specs=in_specs, out_specs=out_specs, check_vma=False
    )
```

profile of v0, /device:TPU:1, one launch (start us, length us, event | category | flops | bytes accessed | tf_op | source)
XLA Modules:
  0.0 1037.5 jit_solution(1986309923351660775)
XLA Ops:
  7.2 1.9 select_select_fusion
  9.2 41.6 %all-gather.4.cloned.1.call-done = f32[1,896,896]{2,1,0:T(8,128)} async-done(((f32[1,112,896]{2,1,0:T(8,128)}), f32[1,896,896]{2,1,0:T(8,128)}) %all-gather.4.cloned.1.call-update) | async-done | bytes 3211280 | tf_op jit(solution)/shard_map/all_gather | solution.py:52
  50.8 176.3 %while.45 = (s32[]{:T(128)}, f32[1,112,896]{2,1,0:T(8,128)S(1)}, f32[1,112,896]{2,1,0:T(8,128)}, f32[1,896,896]{2,1,0:T(8,128)}, s32[]{:T(128)}, /*index=5*/s32[]{:T(128)}, s32[]{:T(128)}, s32[]{:T(128)}) while((s32[]{:T(128)}, f32[1,112,896]{2,1,0:T(8,128)S(1)}, f32[1,112,896]{2,1,0:T(8,128)}, f32[1,896,896]{2,1,0:T(8,128)}, ...), condition=%wide.region_2.3_spmd.clone, body=%wide.region_0.2_spmd.clone.sunk | while | flops 3311623 | bytes 1799325 | solution.py:32
  62.0 1.3 add_reduce_fusion.7
  65.1 1.3 add_reduce_fusion.7
  68.3 1.3 add_reduce_fusion.7
  71.4 1.3 add_reduce_fusion.7
  228.1 35.5 %all-gather.6.cloned.1.call-done = f32[1,896,896]{2,1,0:T(8,128)} async-done(((f32[1,112,896]{2,1,0:T(8,128)}), f32[1,896,896]{2,1,0:T(8,128)}) %all-gather.6.cloned.1.call-update) | async-done | bytes 3211280 | tf_op jit(solution)/shard_map/all_gather | solution.py:52
  263.6 176.1 %while.46 = (s32[]{:T(128)}, f32[1,112,896]{2,1,0:T(8,128)S(1)}, f32[1,112,896]{2,1,0:T(8,128)}, f32[1,896,896]{2,1,0:T(8,128)}, s32[]{:T(128)}, /*index=5*/s32[]{:T(128)}, s32[]{:T(128)}, s32[]{:T(128)}) while((s32[]{:T(128)}, f32[1,112,896]{2,1,0:T(8,128)S(1)}, f32[1,112,896]{2,1,0:T(8,128)}, f32[1,896,896]{2,1,0:T(8,128)}, ...), condition=%wide.region_5.6_spmd.clone, body=%wide.region_3.5_spmd.clone.sunk | while | flops 3311623 | bytes 1799325 | solution.py:32
  439.7 113.6 %gather_fusion.1 = f32[14336]{0:T(1024)S(1)} fusion(f32[112,896]{1,0:T(8,128)S(1)} %bitcast.64, s32[14336]{0:T(1024)S(1)} %or_bitcast_fusion.1), kind=kCustom, calls=%fused_computation.1 | custom fusion | bytes 229376 | tf_op jit(solution)/shard_map/jit(take_along_axis)/gather | solution.py:57
  553.4 104.5 %gather_fusion.2 = f32[16384]{0:T(1024)S(1)} fusion(f32[112,128]{1,0:T(8,128)S(1)} %fusion.8, s32[16384]{0:T(1024)S(1)} %or_bitcast_fusion), kind=kCustom, calls=%fused_computation.2 | custom fusion | bytes 262144 | tf_op jit(solution)/shard_map/jit(take_along_axis)/gather | solution.py:62
  658.8 36.6 %reduce-scatter.2.cloned.1.call-done = f32[1,16,128]{2,1,0:T(8,128)} async-done(((f32[1,128,128]{2,1,0:T(8,128)}), f32[1,16,128]{2,1,0:T(8,128)}) %reduce-scatter.2.cloned.1.call-update) | async-done | bytes 8208 | tf_op jit(solution)/shard_map/reduce_scatter | solution.py:68
  695.4 1.7 reshape.692
  697.1 2.7 copy.15
  699.8 199.1 %all-gather.8.cloned.1.call-done = f32[512,16,128]{2,1,0:T(8,128)} async-done(((f32[1,16,128]{2,1,0:T(8,128)}), f32[512,16,128]{2,1,0:T(8,128)}) %all-gather.8.cloned.1.call-update) | async-done | bytes 4194320 | tf_op jit(solution)/shard_map/all_gather | solution.py:69
  898.9 130.8 %while.44 = (s32[]{:T(128)}, f32[16,64,128]{2,0,1:T(8,128)S(1)}, bf16[16,512,16]{2,0,1:T(8,128)(2,1)}, f32[512,16,128]{2,1,0:T(8,128)}, s32[]{:T(128)}, /*index=5*/s32[]{:T(128)}, s32[]{:T(128)}, s32[]{:T(128)}) while((s32[]{:T(128)}, f32[16,64,128]{2,0,1:T(8,128)S(1)}, bf16[16,512,16]{2,0,1:T(8,128)(2,1)}, f32[512,16,128]{2,1,0:T(8,128)}, ...), condition=%wide.region_10.11_spmd, body=%wide.region_7.10_spmd.sunk | while | flops 2116358 | bytes 2544471 | solution.py:84
  900.0 2.2 gather_fusion
  902.4 2.8 add_reduce_fusion.6
  905.3 1.8 scatter_fusion
  908.1 2.2 gather_fusion
  910.6 2.8 add_reduce_fusion.6
  913.5 1.8 scatter_fusion
  916.3 2.2 gather_fusion
  918.7 2.8 add_reduce_fusion.6
  921.7 1.8 scatter_fusion
  924.5 2.2 gather_fusion
  926.9 2.8 add_reduce_fusion.6
  929.8 1.8 scatter_fusion
  932.7 2.2 gather_fusion
  935.1 2.8 add_reduce_fusion.6
  938.0 1.8 scatter_fusion
  940.8 2.2 gather_fusion
  943.2 2.8 add_reduce_fusion.6
  946.2 1.8 scatter_fusion
  949.0 2.2 gather_fusion
  951.4 2.8 add_reduce_fusion.6
  954.4 1.8 scatter_fusion
  957.2 2.2 gather_fusion
  959.6 2.8 add_reduce_fusion.6
  962.5 1.8 scatter_fusion
  965.4 2.2 gather_fusion
  967.8 2.8 add_reduce_fusion.6
  970.7 1.8 scatter_fusion
  973.5 2.2 gather_fusion
  975.9 2.8 add_reduce_fusion.6
  978.9 1.8 scatter_fusion
  981.7 2.2 gather_fusion
  984.1 2.8 add_reduce_fusion.6
  987.1 1.8 scatter_fusion
  989.9 2.2 gather_fusion
  992.3 2.8 add_reduce_fusion.6
  995.2 1.8 scatter_fusion
  998.1 2.2 gather_fusion
  1000.5 2.8 add_reduce_fusion.6
  1003.4 1.8 scatter_fusion
  1006.2 2.2 gather_fusion
  1008.6 2.8 add_reduce_fusion.6
  1011.6 1.8 scatter_fusion
  1014.4 2.2 gather_fusion
  1016.8 2.8 add_reduce_fusion.6
  1019.8 1.8 scatter_fusion
  1022.6 2.2 gather_fusion
  1025.0 2.8 add_reduce_fusion.6
  1027.9 1.8 scatter_fusion
  (589 shorter events, 367.6 us)
Async XLA Ops:
  6.5 44.3 %all-gather.4.cloned.1.call-start = ((), (), s32[]{:S(2)}) async-start(), calls=%async_computation.1 | async-start | bytes 3612672 | tf_op jit(solution)/shard_map/all_gather | solution.py:52
  9.2 254.4 %all-gather.6.cloned.1.call-start = ((), (), s32[]{:S(2)}) async-start(), calls=%async_computation.2 | async-start | bytes 3612672 | tf_op jit(solution)/shard_map/all_gather | solution.py:52
  50.8 177.1 %copy-start.3 = (s32[1,128]{1,0:T(1,128)S(1)}, s32[1,128]{1,0:T(1,128)}, u32[]{:S(2)}) copy-start(s32[1,128]{1,0:T(1,128)} %param.12) | copy-start | bytes 1540
  227.1 0.8 copy-start
  227.9 467.5 %reduce-scatter.2.cloned.1.call-start = ((), (), s32[]{:S(2)}) async-start(), calls=%async_computation.3 | async-start | bytes 73728 | tf_op jit(solution)/shard_map/reduce_scatter | solution.py:68
  553.3 142.1 %copy-start.1 = (bf16[1,16,8192]{2,1,0:T(8,128)(2,1)S(1)}, bf16[1,16,8192]{2,1,0:T(8,128)(2,1)}, u32[]{:S(2)}) copy-start(bf16[1,16,8192]{2,1,0:T(8,128)(2,1)} %param.13) | copy-start | bytes 786436
  658.7 240.2 %all-gather.8.cloned.1.call-start = ((), (), s32[]{:S(2)}) async-start(), calls=%async_computation.4 | async-start | bytes 4202496 | tf_op jit(solution)/shard_map/all_gather | solution.py:69
  898.9 130.8 %copy-start.2 = (f32[1,16,128]{2,1,0:T(8,128)S(1)}, f32[1,16,128]{2,1,0:T(8,128)}, u32[]{:S(2)}) copy-start(f32[1,16,128]{2,1,0:T(8,128)} %reduce-scatter.2.cloned.1.call-done) | copy-start | bytes 24580
Sparse Core Ops, SparseCore 0:
  9.5 41.2 all-gather.3
  228.0 35.5 all-gather.5
  658.8 36.5 reduce-scatter.1
  699.8 199.0 all-gather.7
where the time goes:
time: 1050 us; the launch traced here: 1040 us
  local copies, waits for them, and re-layouts  472 us (45%)
  waiting for transfers between devices  313 us (30%)
  other arithmetic  233 us (22%)
  between operations  14 us (1%)
    all_gather x1, waiting for transfers between devices, per_device(): portion = lax.all_gather(own_rows, ('cell', 'help'), axis=0, tiled=True)  199 us
    add x224, local copies, waits for them, and re-layouts, relax_one_block(): left_terms[:, :, :, None] + right_terms[:, None, :, :]  193 us
    reduce_min x112, other arithmetic, relax_one_block(): jnp.min(left_terms[:, :, :, None] + right_terms[:, None, :, :], axis=2)  143 us
    gather x1, local copies, waits for them, and re-layouts, per_device(): picked = jnp.take_along_axis(current, expanded, axis=2)  114 us
    gather x1, local copies, waits for them, and re-layouts, per_device(): gathered = jnp.take_along_axis(picked, row_index, axis=1)  105 us
    all_gather x2, waiting for transfers between devices, per_device(): lax.all_gather(current, 'help', axis=1, tiled=True)  77 us
    reduce_min x16, other arithmetic, make_one_block(): jnp.min(left_terms[:, :, :, None] + right_terms[None, :, :, :], axis=2)  44.2 us
    reduce_scatter x1, waiting for transfers between devices, per_device(): own_rows = lax.psum_scatter(placed, 'help', scatter_dimension=1, tiled=True)  36.6 us
  transfers between devices with their start and end apart: 4, of which 4 were waited for; matrix products, arithmetic and copies ran while one was open for 0% of the time, Pallas kernels for 0%

commit v1 on v0

v1 whole, which is shorter than its diff:
```python
import jax
import jax.numpy as jnp
from jax import lax
from jax.experimental import pallas as pl
from jax.experimental.pallas import tpu as pltpu
from jax.sharding import PartitionSpec as P

F32 = jnp.float32
BIG = 1048576.0
SCALE = 0.00390625
NZ, NY, NX = 16, 4, 4
H = 8
CAP = 896
ROWS = 112
PB = 128
SH = 16
L = 16
G = CAP // L
MESH = pl.DeviceIdType.MESH


def slot_cell(h, jj):
    x, c, y, b = h // 2, h % 2, jj // 2, jj % 2
    return (4 * (c + 2 * b) + (x - y) % 4) * NY + y


def lanes(shape):
    return lax.broadcasted_iota(jnp.int32, shape, 1)


def spread(tile, q):
    index = L * q + lanes(tile.shape) % L
    return jnp.take_along_axis(tile, index, axis=1, mode="promise_in_bounds")


def to_rows(block, count):
    turned = jnp.transpose(block)
    lane = lanes((L, PB))
    row = lax.broadcasted_iota(jnp.int32, (L, PB), 0)
    out = []
    for k in range(count):
        part = jnp.zeros((L, PB), F32)
        for q in range(PB // L):
            piece = turned[L * q : L * q + L, :]
            shift = (L * (q - k)) % PB
            if shift:
                piece = pltpu.roll(piece, shift, 1)
            part = jnp.where(lane // L == q, piece, part)
        out.append(jnp.where(lane % L >= row, part, pltpu.roll(part, L, 1)))
    return out


def fold(parts):
    lane = lanes(parts[0].shape)
    d = L // 2
    while d:
        merged = []
        for s in range(d):
            mask = (lane + (2 * PB - s)) % (2 * d) < d
            a = jnp.where(mask, parts[s], parts[s + d])
            b = jnp.where(mask, parts[s + d], parts[s])
            merged.append(jnp.minimum(a, pltpu.roll(b, PB - d, 1)))
        parts = merged
        d //= 2
    return parts[0]


def kernel(
    w_ref, count_ref, sel_ref, selv_ref, cut_ref, o_ref,
    wd, wexp, ablk, abuf, a1, b1r, bnat, a2p, a2r, a2c, a2exp, b2r, piece, cutf, cutr, cutexp, ch, outb,
    s_a, r_a, s_b, r_b, s_p, r_p, s_c, r_c, s_cut, r_cut, s_z, r_z, s_y, r_y, s_o, r_o, l_o,
):
    cell = lax.axis_index("cell")
    me = lax.axis_index("help")
    z, y = cell // NY, cell % NY
    x, core = me // 2, me % 2
    home = 2 * ((z + y) % 4) + (z // 4) % 2
    at_home = home == me
    count = count_ref[0]

    def dev(c, h):
        return {"cell": c, "help": h}

    def peer(r):
        return lax.rem(me + r, H)

    def source_z(b):
        return 4 * (core + 2 * b) + lax.rem(x - y + 4, 4)

    barrier = pltpu.get_barrier_semaphore()

    def greet(c, h):
        pl.semaphore_signal(barrier, inc=1, device_id=dev(c, h), device_id_type=MESH)

    for r in range(1, H):
        greet(cell, peer(r))
    for r in range(1, NY):
        greet(z * NY + lax.rem(y + r, NY), me)
    for b in range(2):
        sz = source_z(b)
        for r in range(H):
            if r:
                greet(sz * NY + y, peer(r))
            else:

                @pl.when(sz != z)
                def _(sz=sz):
                    greet(sz * NY + y, me)

    first = me * ROWS
    shape = (ROWS, PB)
    row = first + lax.broadcasted_iota(jnp.int32, shape, 0)
    tiles = []
    for k in range(CAP // PB):
        t = jnp.where(lanes(shape) + PB * k == row, 0.0, w_ref[0, :, PB * k : PB * k + PB])
        wd[:, PB * k : PB * k + PB] = t
    for h in range(H):
        k, off = (ROWS * h) // PB, (ROWS * h) % PB
        t = wd[:, PB * k : PB * k + PB]
        if off:
            t = pltpu.roll(t, PB - off, 1)
            if off + ROWS > PB:
                n = pltpu.roll(wd[:, PB * k + PB : PB * k + 2 * PB], PB - off, 1)
                t = jnp.where(lanes(shape) < PB - off, t, n)
        ablk[h] = t
    abuf[pl.ds(first, ROWS), :] = ablk[me]
    target = jnp.broadcast_to(selv_ref[...], shape)
    nat = jnp.full(shape, BIG, F32)
    for k in range(CAP // PB):
        got = jnp.take_along_axis(
            wd[:, PB * k : PB * k + PB], target % PB, axis=1, mode="promise_in_bounds"
        )
        nat = jnp.where(target // PB == k, got, nat)
    bnat[0:ROWS, :] = jnp.where(row < count, nat, BIG)
    bnat[ROWS:PB, :] = jnp.full((PB - ROWS, PB), BIG, F32)
    for k, rows in enumerate(to_rows(bnat[...], ROWS // L)):
        b1r[pl.ds(first + L * k, L), :] = rows

    pl.semaphore_wait(barrier, H - 1 + NY - 1 + NZ - jnp.where(at_home, 1, 0))

    def remote(src, dst, ss, rs, c, h):
        return pltpu.make_async_remote_copy(
            src_ref=src, dst_ref=dst, send_sem=ss, recv_sem=rs, device_id=dev(c, h), device_id_type=MESH
        )

    mine = pl.ds(first, ROWS)
    send_a = [
        remote(ablk.at[peer(r)], abuf.at[mine], s_a.at[r], r_a.at[r], cell, peer(r)) for r in range(1, H)
    ]
    for c in send_a:
        c.start()
    send_b = [remote(b1r.at[mine], b1r.at[mine], s_b.at[r], r_b.at[r], cell, peer(r)) for r in range(1, H)]
    for c in send_b:
        c.start()

    for g in range(G):
        k, q = g // 8, g % 8
        wexp[g] = spread(wd[:, PB * k : PB * k + PB], q)
    a_row = me * SH + lax.broadcasted_iota(jnp.int32, (SH, PB), 0)
    for h in range(H):
        for jj in range(8):
            j = slot_cell(h, jj)
            t = cut_ref[0, :, PB * j : PB * j + PB].astype(F32)
            cutf[h, jj] = jnp.where((lanes((SH, PB)) == a_row) & (cell == j), 0.0, t)

    for c in send_a:
        c.wait()

    def pick(i, carry):
        a1[pl.ds(i, 1), :] = abuf[pl.ds(sel_ref[0, i], 1), :]
        return carry

    lax.fori_loop(0, PB, pick, 0)
    col = first + lanes((PB, PB))
    a1[...] = jnp.where(col < count, a1[...], BIG)

    send_p = []
    for i in range(NX):
        chip = lax.rem(x + 1 + i, NX)
        s0 = pl.multiple_of(chip * 2 * SH, 2 * SH)
        left = a1[pl.ds(s0, 2 * SH), :]
        acc = jnp.full((2 * SH, CAP), BIG, F32)
        for w in range(ROWS):
            acc = jnp.minimum(acc, left[:, w : w + 1] + wd[w : w + 1, :])
        a2p[pl.ds(s0, 2 * SH), :] = acc
        for cc in range(2) if i < NX - 1 else (None,):
            dst_core = 1 - core if cc is None else cc
            n = 2 * i + (cc or 0)
            c = remote(
                a2p.at[pl.ds(pl.multiple_of(s0 + SH * dst_core, SH), SH)],
                a2r.at[2 * i + core] if cc is not None else a2r.at[2 * i],
                s_p.at[n],
                r_p.at[2 * i + core] if cc is not None else r_p.at[2 * i],
                cell,
                2 * chip + dst_core,
            )
            c.start()
            send_p.append(c)

    for c in send_b:
        c.wait()

    def contract(expanded, rows, groups):
        def step(g, acc):
            e = expanded(g)
            return tuple(jnp.minimum(acc[s], e + rows(g, s)) for s in range(L))

        return fold(list(lax.fori_loop(0, groups, step, tuple(jnp.full((SH, PB), BIG, F32) for _ in range(L)))))

    def two_arcs(k, carry):
        u0 = pl.multiple_of(k * SH, SH)
        got = contract(lambda g: wexp[g, pl.ds(u0, SH), :], lambda g, s: b1r[pl.ds(g * L + s, 1), :], G)
        u = first + u0 + lax.broadcasted_iota(jnp.int32, (SH, PB), 0)
        bnat[pl.ds(u0, SH), :] = jnp.where(u < count, got, BIG)
        return carry

    lax.fori_loop(0, ROWS // SH, two_arcs, 0)
    for k, rows in enumerate(to_rows(bnat[...], ROWS // L)):
        b2r[pl.ds(first + L * k, L), :] = rows
    send_c = [remote(b2r.at[mine], b2r.at[mine], s_c.at[r], r_c.at[r], cell, peer(r)) for r in range(1, H)]
    for c in send_c:
        c.start()
    send_cut = [
        remote(cutf.at[peer(r)], cutr.at[me], s_cut.at[r], r_cut.at[r], cell, peer(r)) for r in range(1, H)
    ]
    for c in send_cut:
        c.start()
    cutr[me] = cutf[me]

    for n in range(7):
        pltpu.make_async_copy(a2r.at[n], a2r.at[n], r_p.at[n]).wait()
    best = a2p[pl.ds(pl.multiple_of(me * SH, SH), SH), :]
    for n in range(7):
        best = jnp.minimum(best, a2r[n])
    a2c[...] = best
    for g in range(G):
        k, q = g // 8, g % 8
        a2exp[g] = spread(a2c[:, PB * k : PB * k + PB], q)
    for c in send_c:
        c.wait()
    bnat[0:SH, :] = contract(lambda g: a2exp[g], lambda g, s: b2r[pl.ds(g * L + s, 1), :], G)
    piece[...] = to_rows(bnat[...], 1)[0]

    b_own = z // 8
    slot_own = 2 * y + b_own
    mine_ch = ch.at[slot_own, pl.ds(pl.multiple_of(me * L, L), L)]
    send_z = []
    for r in range(NZ):
        c = remote(piece, mine_ch, s_z.at[r], r_z.at[b_own * H + me], lax.rem(z + r, NZ) * NY + y, home)
        if r:
            c.start()
        else:

            @pl.when(home != me)
            def _(c=c):
                c.start()

            @pl.when(home == me)
            def _():
                pltpu.make_async_copy(piece, mine_ch, r_z.at[b_own * H + me]).start()

        send_z.append(c)

    for c in send_cut:
        c.wait()

    def widen(n, carry):
        src, jj = n // 8, n % 8
        t = cutr[src, jj]
        for g in range(8):
            cutexp[src, jj, g] = spread(t, g)
        return carry

    lax.fori_loop(0, 64, widen, 0)

    def near(yy):
        d = lax.rem(z - (4 * core + lax.rem(x - yy + 4, 4)) + NZ, NZ)
        return jnp.where((d <= 4) | (d >= 12), 0, 1)

    def parent(jj):
        def one(src, carry):
            got = contract_few(src)
            outb[jj, src] = got * SCALE
            return carry

        def contract_few(src):
            acc = [jnp.full((SH, PB), BIG, F32) for _ in range(L)]
            for g in range(8):
                e = cutexp[src, jj, g]
                for s in range(L):
                    acc[s] = jnp.minimum(acc[s], e + ch[jj, pl.ds(g * L + s, 1), :])
            return fold(acc)

        lax.fori_loop(0, H, one, 0)
        yy, b = jj // 2, lax.rem(jj, 2)
        j = (4 * (core + 2 * b) + lax.rem(x - yy + 4, 4)) * NY + yy
        where = o_ref.at[:, pl.ds(pl.multiple_of(j * PB, PB), PB)]
        for r in range(1, H):
            remote(outb.at[jj, peer(r)], where, s_o.at[r], r_o.at[r], cell, peer(r)).start()
        pltpu.make_async_copy(outb.at[jj, me], where, l_o).start()

    send_y = []
    b_first = near(y)
    for n in range(2):
        b = b_first if n == 0 else 1 - b_first
        jj = 2 * y + b
        for g in range(H):
            part = ch.at[jj, pl.ds(g * L, L)]
            pltpu.make_async_copy(part, part, r_z.at[b * H + g]).wait()
        for r in range(1, NY):
            c = remote(
                ch.at[jj], ch.at[jj], s_y.at[n * NY + r], r_y.at[n * NY + r],
                z * NY + lax.rem(y + r, NY), me,
            )
            c.start()
            send_y.append(c)
        parent(jj)
    for n in range(2):
        for r in range(1, NY):
            yy = lax.rem(y - r + NY, NY)
            b_src = near(yy)
            jj = 2 * yy + (b_src if n == 0 else 1 - b_src)
            pltpu.make_async_copy(ch.at[jj], ch.at[jj], r_y.at[n * NY + r]).wait()
            parent(jj)

    for c in send_p:
        c.wait_send()
    for r, c in enumerate(send_z):
        if r:
            c.wait_send()
        else:

            @pl.when(home != me)
            def _(c=c):
                c.wait_send()

    for c in send_y:
        c.wait_send()
    for r in range(1, H):
        pltpu.make_async_copy(cutf.at[0], cutf.at[0], s_o.at[r]).wait()
        pltpu.make_async_copy(cutf.at[0], cutf.at[0], r_o.at[r]).wait()
    pltpu.make_async_copy(cutf.at[0], cutf.at[0], l_o).wait()


def per_device(weights, counts, select, cut_weights):
    vmem = pl.BlockSpec(memory_space=pltpu.VMEM)
    smem = pl.BlockSpec(memory_space=pltpu.SMEM)

    def v(*shape):
        return pltpu.VMEM(shape, F32)

    def sem(n):
        return pltpu.SemaphoreType.DMA((n,))

    out = pl.pallas_call(
        kernel,
        out_shape=jax.ShapeDtypeStruct((SH, NZ * NY * PB), F32),
        in_specs=[vmem, smem, smem, vmem, vmem],
        out_specs=pl.BlockSpec(memory_space=pl.ANY),
        scratch_shapes=[
            v(ROWS, CAP),
            v(G, ROWS, PB),
            v(H, ROWS, PB),
            v(CAP, PB),
            v(PB, PB),
            v(CAP, PB),
            v(PB, PB),
            v(PB, CAP),
            v(7, SH, CAP),
            v(SH, CAP),
            v(G, SH, PB),
            v(CAP, PB),
            v(SH, PB),
            v(H, 8, SH, PB),
            v(H, 8, SH, PB),
            v(H, 8, 8, SH, PB),
            v(8, PB, PB),
            v(8, H, SH, PB),
            sem(H), sem(H), sem(H), sem(H), sem(H), sem(H), sem(H), sem(H), sem(H), sem(H),
            sem(NZ), sem(2 * H), sem(2 * NY), sem(2 * NY), sem(H), sem(H), pltpu.SemaphoreType.DMA,
        ],
        compiler_params=pltpu.CompilerParams(
            collective_id=0, has_side_effects=True, vmem_limit_bytes=48 * 1024 * 1024
        ),
    )(weights, counts, select, select, cut_weights)
    return out[None]


def solution(mesh):
    in_specs = (P("cell", "help", None), P("cell"), P("cell", None), P("cell", "help", None))
    return jax.shard_map(
        per_device, mesh=mesh, in_specs=in_specs, out_specs=P("cell", "help", None), check_vma=False
    )
```

time: 1050 us -> 93.3 us (0.09); the launches traced: 1040 us -> 93.1 us
  local copies, waits for them, and re-layouts: 472 us -> 2.74 us
  waiting for transfers between devices: 313 us -> 0 us
  other arithmetic: 233 us -> 0 us
  Pallas kernels: 0 us -> 89.7 us
  between operations: 14 us -> 0.69 us
    all_gather x3 -> x0, waiting for transfers between devices: 276 us -> none  [the longest x1 199 us: per_device(): portion = lax.all_gather(own_rows, ('cell', 'help'), axis=0, tiled=True)]
    gather x18 -> x0, local copies, waits for them, and re-layouts: 253 us -> none  [the longest x1 114 us: per_device(): picked = jnp.take_along_axis(current, expanded, axis=2)]
    add x224 -> x0, local copies, waits for them, and re-layouts: 193 us -> none  [relax_one_block(): left_terms[:, :, :, None] + right_terms[:, None, :, :]]
    reduce_min x128 -> x0, other arithmetic: 188 us -> none  [the longest x112 143 us: relax_one_block(): jnp.min(left_terms[:, :, :, None] + right_terms[:, None, :, :], axis=2)]
    pallas_call x0 -> x1, Pallas kernels: none -> 89.7 us  [per_device(): pl.pallas_call(kernel, out_shape=jax.ShapeDtypeStruct((SH, NZ * NY * PB),...]
    reduce_scatter x1 -> x0, waiting for transfers between devices: 36.6 us -> none  [per_device(): own_rows = lax.psum_scatter(placed, 'help', scatter_dimension=1, tiled=True)]
    another operation x16 -> x0, other arithmetic: 28.6 us -> none  [make_one_block(): return current_best.at[:, owners, :].min(best_paths)]
    dynamic_slice x16 -> x0, local copies, waits for them, and re-layouts: 15.6 us -> none  [make_one_block(): lax.dynamic_slice_in_dim(portion, block_index * blocks, blocks, 0)]
  transfers between devices with their start and end apart: 4 -> 0, of which waited for: 4 -> 0; matrix products, arithmetic and copies ran while one was open for 0% -> 0% of each run, Pallas kernels for 0% -> 0%
where the time goes in v1:
time: 93.3 us; the launch traced here: 93.1 us
  Pallas kernels  89.7 us (96%)
  local copies, waits for them, and re-layouts  2.74 us (3%)
    pallas_call x1, Pallas kernels, per_device(): pl.pallas_call(kernel, out_shape=jax.ShapeDtypeStruct((SH, NZ * NY * PB),...  89.7 us
    unnamed x7, local copies, waits for them, and re-layouts  2.74 us

profile of v1, /device:TPU:1, one launch (start us, length us, event | category | flops | bytes accessed | tf_op | source)
XLA Modules:
  0.0 93.1 jit_solution(3968772924635671085)
XLA Ops:
  0.0 0.0 copy-start.2
  0.7 0.0 copy-done.2
  0.7 0.0 copy-start
  0.7 1.0 %copy-done = f32[1,112,896]{2,1,0:T(8,128)S(1)} copy-done((f32[1,112,896]{2,1,0:T(8,128)S(1)}, f32[1,112,896]{2,1,0:T(8,128)}, u32[]{:S(2)}) %copy-start) | copy-done | bytes 401432
  1.7 0.0 copy-start.1
  1.7 0.9 %copy-done.1 = bf16[1,16,8192]{2,1,0:T(8,128)(2,1)S(1)} copy-done((bf16[1,16,8192]{2,1,0:T(8,128)(2,1)S(1)}, bf16[1,16,8192]{2,1,0:T(8,128)(2,1)}, u32[]{:S(2)}) %copy-start.1) | copy-done | bytes 262168
  2.6 89.7 %shard_map.46 = f32[16,8192]{1,0:T(8,128)S(1)} custom-call(f32[1,112,896]{2,1,0:T(8,128)S(1)} %copy-done, s32[1]{0:T(128)S(6)} %copy.6.count_ref, s32[1,128]{1,0:T(1,128)S(1)} %copy-done.2, s32[1,128]{1,0:T(1,128)S(1)} %copy-done.2, bf16[1,16,8192]{2,1,0:T(8,128)(2,1)S(1)} %copy-done.1), custom_call_target="tpu_custom_call" | custom-call | tf_op jit(solution)/shard_map/pallas_call | solution.py:355
  92.3 0.8 copy.7
Async XLA Ops:
  0.0 0.7 copy-start.2
  0.7 1.0 %copy-start = (f32[1,112,896]{2,1,0:T(8,128)S(1)}, f32[1,112,896]{2,1,0:T(8,128)}, u32[]{:S(2)}) copy-start(f32[1,112,896]{2,1,0:T(8,128)} %w_ref.1) | copy-start | bytes 1204228
  1.7 0.9 %copy-start.1 = (bf16[1,16,8192]{2,1,0:T(8,128)(2,1)S(1)}, bf16[1,16,8192]{2,1,0:T(8,128)(2,1)}, u32[]{:S(2)}) copy-start(bf16[1,16,8192]{2,1,0:T(8,128)(2,1)} %cut_ref.1) | copy-start | bytes 786436

commit v2 on v1

v2 whole, which is shorter than its diff:
```python
import jax
import jax.numpy as jnp
from jax import lax
from jax.experimental import pallas as pl
from jax.experimental.pallas import tpu as pltpu
from jax.sharding import PartitionSpec as P

F32 = jnp.float32
BIG = 1048576.0
SCALE = 0.00390625
NZ, NY, NX = 16, 4, 4
H = 8
CAP = 896
ROWS = 112
PB = 128
SH = 16
L = 16
G = CAP // L
MESH = pl.DeviceIdType.MESH


def slot_cell(h, jj):
    x, c, y, b = h // 2, lax.rem(h, 2), jj // 2, lax.rem(jj, 2)
    return (4 * (c + 2 * b) + lax.rem(x - y + 4, 4)) * NY + y


def lanes(shape):
    return lax.broadcasted_iota(jnp.int32, shape, 1)


def spread(tile, q):
    index = L * q + (lanes(tile.shape) & (L - 1))
    return jnp.take_along_axis(tile, index, axis=1, mode="promise_in_bounds")


def to_rows(block, count):
    turned = jnp.transpose(block)
    lane = lanes((L, PB))
    row = lax.broadcasted_iota(jnp.int32, (L, PB), 0)
    out = []
    for k in range(count):
        part = jnp.zeros((L, PB), F32)
        for q in range(PB // L):
            piece = turned[L * q : L * q + L, :]
            shift = (L * (q - k)) % PB
            if shift:
                piece = pltpu.roll(piece, shift, 1)
            part = jnp.where(lane >> 4 == q, piece, part)
        out.append(jnp.where((lane & (L - 1)) >= row, part, pltpu.roll(part, L, 1)))
    return out


def fold(parts):
    lane = lanes(parts[0].shape)
    d = L // 2
    while d:
        merged = []
        for s in range(d):
            mask = ((lane - s) & d) == 0
            a = jnp.where(mask, parts[s], parts[s + d])
            b = jnp.where(mask, parts[s + d], parts[s])
            merged.append(jnp.minimum(a, pltpu.roll(b, PB - d, 1)))
        parts = merged
        d //= 2
    return parts[0]


def kernel(
    w_ref, count_ref, sel_ref, selv_ref, cut_ref, o_ref,
    wd, wexp, ablk, abuf, a1, b1r, bnat, accb, a2p, a2q, a2r, a2c, a2exp, b2r, piece, cutb, selb, units, cutf, cutr, cutexp,
    ch, outb,
    s_a, r_a, s_b, r_b, s_bf, r_bf, s_q, r_q, s_p, r_p, s_c, r_c, s_cf, r_cf, s_cut, r_cut, s_z, r_z, s_f, r_f, s_y, r_y,
    s_o, r_o, l_o, l_in,
):
    cell = lax.axis_index("cell")
    me = lax.axis_index("help")
    z, y = cell // NY, cell % NY
    x, core = me // 2, me % 2
    home = 2 * ((z + y) % 4) + (z // 4) % 2
    at_home = home == me
    count = count_ref[0]

    def dev(c, h):
        return {"cell": c, "help": h}

    def peer(r):
        return lax.rem(me + r, H)

    def source_z(b):
        return 4 * (core + 2 * b) + lax.rem(x - y + 4, 4)

    loads = [
        pltpu.make_async_copy(w_ref.at[0], wd, l_in.at[0]),
        pltpu.make_async_copy(selv_ref, selb, l_in.at[1]),
        pltpu.make_async_copy(cut_ref.at[0], cutb, l_in.at[2]),
    ]
    for c in loads:
        c.start()

    barrier = pltpu.get_barrier_semaphore()

    def greet(c, h):
        pl.semaphore_signal(barrier, inc=1, device_id=dev(c, h), device_id_type=MESH)

    def along(zz):
        return lax.rem(zz + NZ, NZ)

    def is_near(d):
        return (d <= 4) | (d >= NZ - 4)

    for r in range(1, 5):
        greet(along(z + r) * NY + y, me)
        greet(along(z - r) * NY + y, me)
    for b in range(2):
        sz = source_z(b)

        @pl.when(is_near(along(z - sz)))
        def _(sz=sz):
            for r in range(1, H):
                greet(sz * NY + y, peer(r))

        @pl.when(is_near(along(z - sz)) & (sz != z))
        def _(sz=sz):
            greet(sz * NY + y, me)

    for r in range(1, NY):
        greet(z * NY + lax.rem(y + r, NY), me)
    for r in range(1, H):
        greet(cell, peer(r))

    first = me * ROWS
    shape = (ROWS, PB)
    row = first + lax.broadcasted_iota(jnp.int32, shape, 0)
    loads[0].wait()
    for k in range(CAP // PB):
        t = jnp.where(lanes(shape) + PB * k == row, 0.0, wd[:, PB * k : PB * k + PB])
        wd[:, PB * k : PB * k + PB] = t
    for h in range(H):
        k, off = (ROWS * h) // PB, (ROWS * h) % PB
        t = wd[:, PB * k : PB * k + PB]
        if off:
            t = pltpu.roll(t, PB - off, 1)
            if off + ROWS > PB:
                n = pltpu.roll(wd[:, PB * k + PB : PB * k + 2 * PB], PB - off, 1)
                t = jnp.where(lanes(shape) < PB - off, t, n)
        ablk[h] = t
    abuf[pl.ds(first, ROWS), :] = ablk[me]
    loads[1].wait()
    target = jnp.broadcast_to(selb[...], shape)
    nat = jnp.full(shape, BIG, F32)
    for k in range(CAP // PB):
        got = jnp.take_along_axis(
            wd[:, PB * k : PB * k + PB], target & (PB - 1), axis=1, mode="promise_in_bounds"
        )
        nat = jnp.where(target >> 7 == k, got, nat)
    bnat[0:ROWS, :] = jnp.where(row < count, nat, BIG)
    bnat[ROWS:PB, :] = jnp.full((PB - ROWS, PB), BIG, F32)
    for k, rows in enumerate(to_rows(bnat[...], ROWS // L)):
        b1r[pl.ds(first + L * k, L), :] = rows

    def widen_w(k, carry):
        t = wd[:, pl.ds(pl.multiple_of(k * PB, PB), PB)]
        for q in range(8):
            wexp[8 * k + q] = spread(t, q)
        return carry

    lax.fori_loop(0, CAP // PB, widen_w, 0)
    unit_row = lax.broadcasted_iota(jnp.int32, (PB, PB), 0)
    for g in range(8):
        units[:, PB * g : PB * g + PB] = jnp.where(
            unit_row == L * g + (lanes((PB, PB)) & (L - 1)), 1.0, 0.0
        ).astype(jnp.bfloat16)

    def clear(k, carry):
        accb[k] = jnp.full((L, SH, PB), BIG, F32)
        return carry

    lax.fori_loop(0, ROWS // SH, clear, 0)
    loads[2].wait()

    pl.semaphore_wait(barrier, H - 1 + NY - 1 + 8 + 9 - jnp.where(at_home, 1, 0))

    def remote(src, dst, ss, rs, c, h):
        return pltpu.make_async_remote_copy(
            src_ref=src, dst_ref=dst, send_sem=ss, recv_sem=rs, device_id=dev(c, h), device_id_type=MESH
        )

    mine = pl.ds(first, ROWS)
    partner = 2 * x + 1 - core

    def rows_of(h):
        return pl.ds(pl.multiple_of(h * ROWS, L), ROWS)

    def share(buf, ss, rs, n):
        to = partner if n == 0 else 2 * lax.rem(x + n, NX) + core
        return remote(buf.at[mine], buf.at[mine], ss.at[n], rs.at[n], cell, to)

    def pass_on(buf, ss, rs, n):
        part = buf.at[rows_of(2 * lax.rem(x - n + NX, NX) + core)]
        return remote(part, part, ss.at[n], rs.at[n], cell, partner)

    for n in (1, 3, 2, 0):
        share(b1r, s_b, r_b, n).start()
    send_a = [
        remote(ablk.at[peer(r)], abuf.at[mine], s_a.at[r], r_a.at[r], cell, peer(r)) for r in range(1, H)
    ]
    for c in send_a:
        c.start()

    a_row = me * SH + lax.broadcasted_iota(jnp.int32, (SH, PB), 0)

    def widen_cut(n, carry):
        h, jj = n // 8, lax.rem(n, 8)
        j = slot_cell(h, jj)
        t = cutb[:, pl.ds(pl.multiple_of(j * PB, PB), PB)].astype(F32)
        cutf[h, jj] = jnp.where((lanes((SH, PB)) == a_row) & (cell == j), 0.0, t)
        return carry

    lax.fori_loop(0, 64, widen_cut, 0, unroll=4)

    send_cut = [
        remote(cutf.at[peer(r)], cutr.at[me], s_cut.at[r], r_cut.at[r], cell, peer(r)) for r in range(1, H)
    ]
    for c in send_cut[0:2]:
        c.start()
    cutr[me] = cutf[me]

    def over_block(n, carry):
        m = lax.rem(n + 1, 3)
        hop = jnp.where(n < 2, 0, jnp.where(m == 0, 1, jnp.where(m == 1, 3, 2)))
        same = (n == 0) | ((n >= 2) & (n < 5))
        src = 2 * lax.rem(x - hop + NX, NX) + jnp.where(same, core, 1 - core)

        @pl.when((n >= 1) & (n < 5))
        def _():
            pltpu.make_async_copy(b1r.at[mine], b1r.at[mine], r_b.at[hop]).wait()

        @pl.when((n >= 2) & (n < 5))
        def _():
            pass_on(b1r, s_bf, r_bf, hop).start()

        @pl.when(n >= 5)
        def _():
            pltpu.make_async_copy(b1r.at[mine], b1r.at[mine], r_bf.at[hop]).wait()

        r0 = pl.multiple_of(src * ROWS, L)

        def rows_u(k, carry):
            u0 = pl.multiple_of(k * SH, SH)
            acc = [accb[k, s] for s in range(L)]
            for q in range(ROWS // L):
                e = wexp[src * (ROWS // L) + q, pl.ds(u0, SH), :]
                for s in range(L):
                    acc[s] = jnp.minimum(acc[s], e + b1r[pl.ds(r0 + (q * L + s), 1), :])
            for s in range(L):
                accb[k, s] = acc[s]
            return carry

        lax.fori_loop(0, ROWS // SH, rows_u, 0)
        return carry

    lax.fori_loop(0, H, over_block, 0)

    def finish(k, carry):
        u0 = pl.multiple_of(k * SH, SH)
        u = first + u0 + lax.broadcasted_iota(jnp.int32, (SH, PB), 0)
        bnat[pl.ds(u0, SH), :] = jnp.where(u < count, fold([accb[k, s] for s in range(L)]), BIG)
        return carry

    lax.fori_loop(0, ROWS // SH, finish, 0, unroll=True)
    for k, rows in enumerate(to_rows(bnat[...], ROWS // L)):
        b2r[pl.ds(first + L * k, L), :] = rows
    for n in (1, 3, 2, 0):
        share(b2r, s_c, r_c, n).start()
    for c in send_cut[2:4]:
        c.start()

    for c in send_a:
        c.wait()

    def pick(i, carry):
        a1[pl.ds(i, 1), :] = abuf[pl.ds(sel_ref[0, i], 1), :]
        return carry

    lax.fori_loop(0, PB, pick, 0, unroll=8)
    col = first + lanes((PB, PB))
    a1[...] = jnp.where(col < count, a1[...], BIG)

    def strip(chip, cc):
        return pl.ds(pl.multiple_of((2 * chip + cc) * SH, SH), SH)

    def cross(i, chip):
        return remote(a2p.at[strip(chip, 1 - core)], a2q.at[i], s_q.at[i], r_q.at[i], cell, partner)

    def merged(i):
        chip = lax.rem(x + 1 + i, NX)
        at = strip(chip, core)
        pltpu.make_async_copy(a2q.at[i], a2q.at[i], r_q.at[i]).wait()
        a2p[at, :] = jnp.minimum(a2p[at, :], a2q[i])
        return remote(a2p.at[at], a2r.at[i], s_p.at[i], r_p.at[i], cell, 2 * chip + core)

    def from_chosen(i, carry):
        chip = lax.rem(x + 1 + i, NX)
        s0 = pl.multiple_of(chip * 2 * SH, 2 * SH)
        left = a1[pl.ds(s0, 2 * SH), :]

        acc = jnp.full((2 * SH, CAP), BIG, F32)
        for w in range(ROWS):
            acc = jnp.minimum(acc, left[:, w : w + 1] + wd[w : w + 1, :])
        a2p[pl.ds(s0, 2 * SH), :] = acc
        cross(i, chip).start()

        @pl.when(i >= 1)
        def _():
            merged(i - 1).start()

        return carry

    lax.fori_loop(0, NX, from_chosen, 0)

    for n in (1, 3, 2):
        pltpu.make_async_copy(b2r.at[mine], b2r.at[mine], r_c.at[n]).wait()
        pass_on(b2r, s_cf, r_cf, n).start()
    for c in send_cut[4:]:
        c.start()
    def contract(expanded, rows, groups):
        def step(k, acc):
            acc = list(acc)
            for q in range(8):
                e = expanded(8 * k + q)
                for s in range(L):
                    acc[s] = jnp.minimum(acc[s], e + rows(k * PB, q * L + s))
            return tuple(acc)

        acc = tuple(jnp.full((SH, PB), BIG, F32) for _ in range(L))
        return fold(list(lax.fori_loop(0, groups // 8, step, acc)))

    for n in range(NX - 1):
        pltpu.make_async_copy(a2r.at[n], a2r.at[n], r_p.at[n]).wait()
    pltpu.make_async_copy(a2q.at[NX - 1], a2q.at[NX - 1], r_q.at[NX - 1]).wait()
    best = jnp.minimum(a2p[strip(x, core), :], a2q[NX - 1])
    for n in range(NX - 1):
        best = jnp.minimum(best, a2r[n])
    a2c[...] = best
    for g in range(G):
        k, q = g // 8, g % 8
        a2exp[g] = spread(a2c[:, PB * k : PB * k + PB], q)
    pltpu.make_async_copy(b2r.at[mine], b2r.at[mine], r_c.at[0]).wait()
    for n in (1, 3, 2):
        pltpu.make_async_copy(b2r.at[mine], b2r.at[mine], r_cf.at[n]).wait()
    bnat[0:SH, :] = contract(lambda g: a2exp[g], lambda r0, r: b2r[pl.ds(pl.multiple_of(r0, PB) + r, 1), :], G)
    piece[...] = to_rows(bnat[...], 1)[0]

    b_own = z // 8
    slot_own = 2 * y + b_own
    mine_ch = ch.at[slot_own, pl.ds(pl.multiple_of(me * L, L), L)]

    def to_home(r):
        return remote(piece, mine_ch, s_z.at[r + 4], r_z.at[b_own * H + me], along(z + r) * NY + y, home)

    for r in (4, -4, 3, -3, 2, -2, 1, -1):
        to_home(r).start()

    @pl.when(home != me)
    def _():
        to_home(0).start()

    @pl.when(home == me)
    def _():
        pltpu.make_async_copy(piece, mine_ch, r_z.at[b_own * H + me]).start()

    for c in send_cut:
        c.wait()

    def widen(src, carry):
        t = cutr[src].reshape(PB, PB).astype(jnp.bfloat16)
        wide = jnp.dot(t, units[...], preferred_element_type=F32)
        for g in range(8):
            cutexp[src, g] = wide[:, PB * g : PB * g + PB]
        return carry

    lax.fori_loop(0, H, widen, 0)

    def from_source(yy, b):
        return along(z - (4 * (core + 2 * b) + lax.rem(x - yy + 4, 4)))

    def near(yy):
        return jnp.where(is_near(from_source(yy, 0)), 0, 1)

    def forward(jj, b, r):
        n = b * 8 + r + 3
        return remote(ch.at[jj], ch.at[jj], s_f.at[n], r_f.at[b], along(z + r) * NY + y, me)

    def parent(jj):
        def one(src, carry):
            got = contract_few(src)
            outb[jj, src] = got * SCALE
            return carry

        def contract_few(src):
            acc = [None] * L
            for g in range(8):
                e = cutexp[src, g, pl.ds(pl.multiple_of(jj * SH, SH), SH), :]
                for s in range(L):
                    sums = e + ch[jj, pl.ds(g * L + s, 1), :]
                    acc[s] = jnp.minimum(acc[s], sums) if g else sums
            return fold(acc)

        lax.fori_loop(0, H, one, 0, unroll=4)
        yy, b = jj // 2, lax.rem(jj, 2)
        j = (4 * (core + 2 * b) + lax.rem(x - yy + 4, 4)) * NY + yy
        where = o_ref.at[:, pl.ds(pl.multiple_of(j * PB, PB), PB)]
        for r in range(1, H):
            remote(outb.at[jj, peer(r)], where, s_o.at[r], r_o.at[r], cell, peer(r)).start()
        pltpu.make_async_copy(outb.at[jj, me], where, l_o).start()

    def along_y(r, jj, which):
        sem = which * NY + r
        return remote(ch.at[jj], ch.at[jj], s_y.at[sem], r_y.at[sem], z * NY + lax.rem(y + r, NY), me)

    def take(b, which):
        jj = 2 * y + b
        d = from_source(y, b)

        @pl.when(is_near(d))
        def _():
            for g in range(H):
                part = ch.at[jj, pl.ds(g * L, L)]
                pltpu.make_async_copy(part, part, r_z.at[b * H + g]).wait()

        @pl.when(jnp.logical_not(is_near(d)))
        def _():
            pltpu.make_async_copy(ch.at[jj], ch.at[jj], r_f.at[b]).wait()

        @pl.when(d == 4)
        def _():
            for k in (4, 3, 2, 1):
                forward(jj, b, k).start()

        @pl.when(d == NZ - 4)
        def _():
            for k in (3, 2, 1):
                forward(jj, b, -k).start()

        for k in range(1, NY):
            along_y(k, jj, which).start()

    b_near = near(y)
    both_near = is_near(from_source(y, 1 - b_near))

    def serve(n, carry):
        which, r = n // NY, lax.rem(n, NY)
        yy = lax.rem(y - r + NY, NY)
        first_b = near(yy)
        b = jnp.where(which == 0, first_b, 1 - first_b)
        jj = 2 * yy + b

        @pl.when(n == 0)
        def _():
            take(b_near, 0)

        @pl.when(((n == 0) & both_near) | ((n == NY) & jnp.logical_not(both_near)))
        def _():
            take(1 - b_near, 1)

        @pl.when(r > 0)
        def _():
            pltpu.make_async_copy(ch.at[jj], ch.at[jj], r_y.at[which * NY + r]).wait()

        parent(jj)
        return carry

    lax.fori_loop(0, 8, serve, 0)

    for n in range(NX):
        pltpu.make_async_copy(a2q.at[0], a2q.at[0], s_q.at[n]).wait()
        if n < NX - 1:
            pltpu.make_async_copy(a2q.at[0], a2q.at[0], s_p.at[n]).wait()
    for n in range(NX):
        share(b1r, s_b, r_b, n).wait_send()
        share(b2r, s_c, r_c, n).wait_send()
        if n:
            pass_on(b1r, s_bf, r_bf, n).wait_send()
            pass_on(b2r, s_cf, r_cf, n).wait_send()
    for r in range(-4, 5):
        if r:
            to_home(r).wait_send()

    @pl.when(home != me)
    def _():
        to_home(0).wait_send()

    for b in range(2):
        d = from_source(y, b)

        @pl.when(d == 4)
        def _(b=b):
            for k in range(1, 5):
                forward(2 * y + b, b, k).wait_send()

        @pl.when(d == NZ - 4)
        def _(b=b):
            for k in range(1, 4):
                forward(2 * y + b, b, -k).wait_send()

    for which in range(2):
        for r in range(1, NY):
            along_y(r, 2 * y, which).wait_send()
    for r in range(1, H):
        pltpu.make_async_copy(cutf.at[0], cutf.at[0], s_o.at[r]).wait()
        pltpu.make_async_copy(cutf.at[0], cutf.at[0], r_o.at[r]).wait()
    pltpu.make_async_copy(cutf.at[0], cutf.at[0], l_o).wait()


def per_device(weights, counts, select, cut_weights):
    hbm = pl.BlockSpec(memory_space=pltpu.HBM)
    smem = pl.BlockSpec(memory_space=pltpu.SMEM)

    def hold(a):
        return pltpu.with_memory_space_constraint(a, pltpu.HBM)

    def v(*shape):
        return pltpu.VMEM(shape, F32)

    def sem(n):
        return pltpu.SemaphoreType.DMA((n,))

    out = pl.pallas_call(
        kernel,
        out_shape=jax.ShapeDtypeStruct((SH, NZ * NY * PB), F32),
        in_specs=[hbm, smem, smem, hbm, hbm],
        out_specs=hbm,
        scratch_shapes=[
            v(ROWS, CAP),
            v(G, ROWS, PB),
            v(H, ROWS, PB),
            v(CAP, PB),
            v(PB, PB),
            v(CAP, PB),
            v(PB, PB),
            v(ROWS // SH, L, SH, PB),
            v(PB, CAP),
            v(NX, SH, CAP),
            v(NX - 1, SH, CAP),
            v(SH, CAP),
            v(G, SH, PB),
            v(CAP, PB),
            v(SH, PB),
            pltpu.VMEM((SH, NZ * NY * PB), jnp.bfloat16),
            pltpu.VMEM((1, PB), jnp.int32),
            pltpu.VMEM((PB, 8 * PB), jnp.bfloat16),
            v(H, 8, SH, PB),
            v(H, 8, SH, PB),
            v(H, 8, PB, PB),
            v(8, PB, PB),
            v(8, H, SH, PB),
            sem(H), sem(H), sem(NX), sem(NX), sem(NX), sem(NX), sem(NX), sem(NX), sem(NX), sem(NX), sem(NX), sem(NX), sem(NX), sem(NX),
            sem(H), sem(H), sem(9), sem(2 * H), sem(16), sem(2), sem(2 * NY), sem(2 * NY), sem(H), sem(H),
            pltpu.SemaphoreType.DMA, sem(3),
        ],
        compiler_params=pltpu.CompilerParams(
            collective_id=0, has_side_effects=True, vmem_limit_bytes=48 * 1024 * 1024
        ),
    )(hold(weights), counts, select, hold(select), hold(cut_weights))
    return out[None]


def solution(mesh):
    in_specs = (P("cell", "help", None), P("cell"), P("cell", None), P("cell", "help", None))
    return jax.shard_map(
        per_device, mesh=mesh, in_specs=in_specs, out_specs=P("cell", "help", None), check_vma=False
    )
```

time: 93.3 us -> 66.9 us (0.72)
  Pallas kernels: 89.7 us -> 65.3 us
  local copies, waits for them, and re-layouts: 2.74 us -> 0.8 us
    pallas_call x1, Pallas kernels: 89.7 us -> 65.3 us  [per_device(): pl.pallas_call(kernel, out_shape=jax.ShapeDtypeStruct((SH, NZ * NY * PB),...]
    unnamed x7 -> x1, local copies, waits for them, and re-layouts: 2.74 us -> 0.8 us
where the time goes in v2:
time: 66.9 us; the launch traced here: 66.7 us
  Pallas kernels  65.3 us (98%)
  local copies, waits for them, and re-layouts  0.8 us (1%)
    pallas_call x1, Pallas kernels, per_device(): pl.pallas_call(kernel, out_shape=jax.ShapeDtypeStruct((SH, NZ * NY * PB),...  65.3 us

profile of v2, /device:TPU:1, one launch (start us, length us, event | category | flops | bytes accessed | tf_op | source)
XLA Modules:
  0.0 66.7 jit_solution(9866285397493537604)
XLA Ops:
  0.7 65.3 %shard_map.46 = f32[16,8192]{1,0:T(8,128)S(1)} custom-call(f32[1,112,896]{2,1,0:T(8,128)} %w_ref.1, s32[1]{0:T(128)S(6)} %copy.6.count_ref, s32[1,128]{1,0:T(1,128)} %selv_ref.1, s32[1,128]{1,0:T(1,128)} %selv_ref.1, bf16[1,16,8192]{2,1,0:T(8,128)(2,1)} %cut_ref.1), custom_call_target="tpu_custom_call" | custom-call | tf_op jit(solution)/shard_map/pallas_call | solution.py:528
  65.9 0.8 %copy.7 = f32[1,16,8192]{2,1,0:T(8,128)} copy(f32[1,16,8192]{2,1,0:T(8,128)S(1)} %bitcast.1) | data formatting | bytes 1048576

commit v3 on v2

--- a/solution.py
+++ b/solution.py
@@ -67,7 +67,7 @@
 
 def kernel(
     w_ref, count_ref, sel_ref, selv_ref, cut_ref, o_ref,
-    wd, wexp, ablk, abuf, a1, b1r, bnat, accb, a2p, a2q, a2r, a2c, a2exp, b2r, piece, cutb, selb, units, cutf, cutr, cutexp,
+    wd, wexp, ablk, abuf, a1, b1r, bnat, accb, a2p, a2q, a2r, a2c, a2exp, b2r, piece, cutb, selb, sels, units, cutf, cutr, cutexp,
     ch, outb,
     s_a, r_a, s_b, r_b, s_bf, r_bf, s_q, r_q, s_p, r_p, s_c, r_c, s_cf, r_cf, s_cut, r_cut, s_z, r_z, s_f, r_f, s_y, r_y,
     s_o, r_o, l_o, l_in,
@@ -78,7 +78,6 @@
     x, core = me // 2, me % 2
     home = 2 * ((z + y) % 4) + (z // 4) % 2
     at_home = home == me
-    count = count_ref[0]
 
     def dev(c, h):
         return {"cell": c, "help": h}
@@ -93,6 +92,7 @@
         pltpu.make_async_copy(w_ref.at[0], wd, l_in.at[0]),
         pltpu.make_async_copy(selv_ref, selb, l_in.at[1]),
         pltpu.make_async_copy(cut_ref.at[0], cutb, l_in.at[2]),
+        pltpu.make_async_copy(sel_ref, sels, l_in.at[3]),
     ]
     for c in loads:
         c.start()
@@ -108,9 +108,6 @@
     def is_near(d):
         return (d <= 4) | (d >= NZ - 4)
 
-    for r in range(1, 5):
-        greet(along(z + r) * NY + y, me)
-        greet(along(z - r) * NY + y, me)
     for b in range(2):
         sz = source_z(b)
 
@@ -123,6 +120,9 @@
         def _(sz=sz):
             greet(sz * NY + y, me)
 
+    for r in (4, 3, 2, 1):
+        greet(along(z + r) * NY + y, me)
+        greet(along(z - r) * NY + y, me)
     for r in range(1, NY):
         greet(z * NY + lax.rem(y + r, NY), me)
     for r in range(1, H):
@@ -146,6 +146,8 @@
         ablk[h] = t
     abuf[pl.ds(first, ROWS), :] = ablk[me]
     loads[1].wait()
+    loads[3].wait()
+    count = count_ref[0]
     target = jnp.broadcast_to(selb[...], shape)
     nat = jnp.full(shape, BIG, F32)
     for k in range(CAP // PB):
@@ -199,7 +201,7 @@
         part = buf.at[rows_of(2 * lax.rem(x - n + NX, NX) + core)]
         return remote(part, part, ss.at[n], rs.at[n], cell, partner)
 
-    for n in (1, 3, 2, 0):
+    for n in (0, 1, 3, 2):
         share(b1r, s_b, r_b, n).start()
     send_a = [
         remote(ablk.at[peer(r)], abuf.at[mine], s_a.at[r], r_a.at[r], cell, peer(r)) for r in range(1, H)
@@ -221,7 +223,7 @@
     send_cut = [
         remote(cutf.at[peer(r)], cutr.at[me], s_cut.at[r], r_cut.at[r], cell, peer(r)) for r in range(1, H)
     ]
-    for c in send_cut[0:2]:
+    for c in send_cut[0:4]:
         c.start()
     cutr[me] = cutf[me]
 
@@ -272,14 +274,14 @@
         b2r[pl.ds(first + L * k, L), :] = rows
     for n in (1, 3, 2, 0):
         share(b2r, s_c, r_c, n).start()
-    for c in send_cut[2:4]:
+    for c in send_cut[4:]:
         c.start()
 
     for c in send_a:
         c.wait()
 
     def pick(i, carry):
-        a1[pl.ds(i, 1), :] = abuf[pl.ds(sel_ref[0, i], 1), :]
+        a1[pl.ds(i, 1), :] = abuf[pl.ds(sels[0, i], 1), :]
         return carry
 
     lax.fori_loop(0, PB, pick, 0, unroll=8)
@@ -321,8 +323,6 @@
     for n in (1, 3, 2):
         pltpu.make_async_copy(b2r.at[mine], b2r.at[mine], r_c.at[n]).wait()
         pass_on(b2r, s_cf, r_cf, n).start()
-    for c in send_cut[4:]:
-        c.start()
     def contract(expanded, rows, groups):
         def step(k, acc):
             acc = list(acc)
@@ -442,14 +442,15 @@
             for k in (3, 2, 1):
                 forward(jj, b, -k).start()
 
-        for k in range(1, NY):
+        for k in (1, 3, 2):
             along_y(k, jj, which).start()
 
     b_near = near(y)
     both_near = is_near(from_source(y, 1 - b_near))
 
     def serve(n, carry):
-        which, r = n // NY, lax.rem(n, NY)
+        which, m = n // NY, lax.rem(n, NY)
+        r = jnp.where(m >= 2, 5 - m, m)
         yy = lax.rem(y - r + NY, NY)
         first_b = near(yy)
         b = jnp.where(which == 0, first_b, 1 - first_b)
@@ -514,7 +515,6 @@
 
 def per_device(weights, counts, select, cut_weights):
     hbm = pl.BlockSpec(memory_space=pltpu.HBM)
-    smem = pl.BlockSpec(memory_space=pltpu.SMEM)
 
     def hold(a):
         return pltpu.with_memory_space_constraint(a, pltpu.HBM)
@@ -528,7 +528,7 @@
     out = pl.pallas_call(
         kernel,
         out_shape=jax.ShapeDtypeStruct((SH, NZ * NY * PB), F32),
-        in_specs=[hbm, smem, smem, hbm, hbm],
+        in_specs=[hbm, pl.BlockSpec(memory_space=pltpu.SMEM), hbm, hbm, hbm],
         out_specs=hbm,
         scratch_shapes=[
             v(ROWS, CAP),
@@ -548,6 +548,7 @@
             v(SH, PB),
             pltpu.VMEM((SH, NZ * NY * PB), jnp.bfloat16),
             pltpu.VMEM((1, PB), jnp.int32),
+            pltpu.SMEM((1, PB), jnp.int32),
             pltpu.VMEM((PB, 8 * PB), jnp.bfloat16),
             v(H, 8, SH, PB),
             v(H, 8, SH, PB),
@@ -556,12 +557,12 @@
             v(8, H, SH, PB),
             sem(H), sem(H), sem(NX), sem(NX), sem(NX), sem(NX), sem(NX), sem(NX), sem(NX), sem(NX), sem(NX), sem(NX), sem(NX), sem(NX),
             sem(H), sem(H), sem(9), sem(2 * H), sem(16), sem(2), sem(2 * NY), sem(2 * NY), sem(H), sem(H),
-            pltpu.SemaphoreType.DMA, sem(3),
+            pltpu.SemaphoreType.DMA, sem(4),
         ],
         compiler_params=pltpu.CompilerParams(
             collective_id=0, has_side_effects=True, vmem_limit_bytes=48 * 1024 * 1024
         ),
-    )(hold(weights), counts, select, hold(select), hold(cut_weights))
+    )(hold(weights), counts, hold(select), hold(select), hold(cut_weights))
     return out[None]
 
 

time: 66.9 us -> 64.8 us (0.969)
  Pallas kernels: 65.3 us -> 62.7 us
    pallas_call x1, Pallas kernels: 65.3 us -> 62.7 us  [per_device(): pl.pallas_call(kernel, out_shape=jax.ShapeDtypeStruct((SH, NZ * NY * PB),...]
where the time goes in v3:
time: 64.8 us; the launch traced here: 64.2 us
  Pallas kernels  62.7 us (97%)
  local copies, waits for them, and re-layouts  0.8 us (1%)
  between operations  0.66 us (1%)
    pallas_call x1, Pallas kernels, per_device(): pl.pallas_call(kernel, out_shape=jax.ShapeDtypeStruct((SH, NZ * NY * PB),...  62.7 us

profile of v3, /device:TPU:1, one launch (start us, length us, event | category | flops | bytes accessed | tf_op | source)
XLA Modules:
  0.0 64.2 jit_solution(17497445449253574122)
XLA Ops:
  0.7 62.7 %shard_map.46 = f32[16,8192]{1,0:T(8,128)S(1)} custom-call(f32[1,112,896]{2,1,0:T(8,128)} %w_ref.1, s32[1]{0:T(128)S(6)} %copy.6.count_ref, s32[1,128]{1,0:T(1,128)} %selv_ref.1, s32[1,128]{1,0:T(1,128)} %selv_ref.1, bf16[1,16,8192]{2,1,0:T(8,128)(2,1)} %cut_ref.1), custom_call_target="tpu_custom_call" | custom-call | tf_op jit(solution)/shard_map/pallas_call | solution.py:528
  63.4 0.8 %copy.7 = f32[1,16,8192]{2,1,0:T(8,128)} copy(f32[1,16,8192]{2,1,0:T(8,128)S(1)} %bitcast.1) | data formatting | bytes 1048576

commit v4 on v3

--- a/solution.py
+++ b/solution.py
@@ -66,10 +66,10 @@
 
 
 def kernel(
-    w_ref, count_ref, sel_ref, selv_ref, cut_ref, o_ref,
-    wd, wexp, ablk, abuf, a1, b1r, bnat, accb, a2p, a2q, a2r, a2c, a2exp, b2r, piece, cutb, selb, sels, units, cutf, cutr, cutexp,
+    w_ref, count_ref, selv_ref, cut_ref, o_ref,
+    wd, wexp, zs, zq, za, a1, b1r, bnat, accb, a2p, a2q, a2r, a2c, a2exp, b2r, piece, cutb, selb, units, cutf, cutr, cutexp,
     ch, outb,
-    s_a, r_a, s_b, r_b, s_bf, r_bf, s_q, r_q, s_p, r_p, s_c, r_c, s_cf, r_cf, s_cut, r_cut, s_z, r_z, s_f, r_f, s_y, r_y,
+    s_zq, r_zq, s_a, r_a, s_b, r_b, s_bf, r_bf, s_q, r_q, s_p, r_p, s_c, r_c, s_cf, r_cf, s_cut, r_cut, s_z, r_z, s_f, r_f, s_y, r_y,
     s_o, r_o, l_o, l_in,
 ):
     cell = lax.axis_index("cell")
@@ -92,7 +92,6 @@
         pltpu.make_async_copy(w_ref.at[0], wd, l_in.at[0]),
         pltpu.make_async_copy(selv_ref, selb, l_in.at[1]),
         pltpu.make_async_copy(cut_ref.at[0], cutb, l_in.at[2]),
-        pltpu.make_async_copy(sel_ref, sels, l_in.at[3]),
     ]
     for c in loads:
         c.start()
@@ -135,6 +134,13 @@
     for k in range(CAP // PB):
         t = jnp.where(lanes(shape) + PB * k == row, 0.0, wd[:, PB * k : PB * k + PB])
         wd[:, PB * k : PB * k + PB] = t
+    loads[1].wait()
+    count = count_ref[0]
+    spot = lax.broadcasted_iota(jnp.int32, (PB, PB), 0)
+    held = (jnp.broadcast_to(selb[...], (PB, PB)) == first + spot) & (spot < ROWS)
+    one = jnp.transpose(jnp.where(held, 1.0, 0.0))
+    owned = jnp.max(one, axis=1, keepdims=True) > 0.5
+    one = one[:, 0:ROWS].astype(jnp.bfloat16)
     for h in range(H):
         k, off = (ROWS * h) // PB, (ROWS * h) % PB
         t = wd[:, PB * k : PB * k + PB]
@@ -143,11 +149,12 @@
             if off + ROWS > PB:
                 n = pltpu.roll(wd[:, PB * k + PB : PB * k + 2 * PB], PB - off, 1)
                 t = jnp.where(lanes(shape) < PB - off, t, n)
-        ablk[h] = t
-    abuf[pl.ds(first, ROWS), :] = ablk[me]
-    loads[1].wait()
-    loads[3].wait()
-    count = count_ref[0]
+        picked = jnp.zeros((PB, PB), F32)
+        for _ in range(3):
+            part = t.astype(jnp.bfloat16)
+            picked = picked + jnp.dot(one, part, preferred_element_type=F32)
+            t = t - part.astype(F32)
+        zs[h] = jnp.where(owned, picked, BIG)
     target = jnp.broadcast_to(selb[...], shape)
     nat = jnp.full(shape, BIG, F32)
     for k in range(CAP // PB):
@@ -160,6 +167,43 @@
     for k, rows in enumerate(to_rows(bnat[...], ROWS // L)):
         b1r[pl.ds(first + L * k, L), :] = rows
 
+    loads[2].wait()
+
+    pl.semaphore_wait(barrier, H - 1 + NY - 1 + 8 + 9 - jnp.where(at_home, 1, 0))
+
+    def remote(src, dst, ss, rs, c, h):
+        return pltpu.make_async_remote_copy(
+            src_ref=src, dst_ref=dst, send_sem=ss, recv_sem=rs, device_id=dev(c, h), device_id_type=MESH
+        )
+
+    mine = pl.ds(first, ROWS)
+    partner = 2 * x + 1 - core
+
+    def rows_of(h):
+        return pl.ds(pl.multiple_of(h * ROWS, L), ROWS)
+
+    def share(buf, ss, rs, n):
+        to = partner if n == 0 else 2 * lax.rem(x + n, NX) + core
+        return remote(buf.at[mine], buf.at[mine], ss.at[n], rs.at[n], cell, to)
+
+    def pass_on(buf, ss, rs, n):
+        part = buf.at[rows_of(2 * lax.rem(x - n + NX, NX) + core)]
+        return remote(part, part, ss.at[n], rs.at[n], cell, partner)
+
+    for n in (0, 1, 3, 2):
+        share(b1r, s_b, r_b, n).start()
+
+    def lend(n):
+        chip = lax.rem(x + n, NX)
+        return remote(zs.at[2 * chip + 1 - core], zq.at[n], s_zq.at[n], r_zq.at[n], cell, partner)
+
+    def ship(n):
+        chip = lax.rem(x + n, NX)
+        return remote(zs.at[2 * chip + core], za.at[n - 1], s_a.at[n], r_a.at[n], cell, 2 * chip + core)
+
+    for n in (2, 1, 3, 0):
+        lend(n).start()
+
     def widen_w(k, carry):
         t = wd[:, pl.ds(pl.multiple_of(k * PB, PB), PB)]
         for q in range(8):
@@ -178,37 +222,6 @@
         return carry
 
     lax.fori_loop(0, ROWS // SH, clear, 0)
-    loads[2].wait()
-
-    pl.semaphore_wait(barrier, H - 1 + NY - 1 + 8 + 9 - jnp.where(at_home, 1, 0))
-
-    def remote(src, dst, ss, rs, c, h):
-        return pltpu.make_async_remote_copy(
-            src_ref=src, dst_ref=dst, send_sem=ss, recv_sem=rs, device_id=dev(c, h), device_id_type=MESH
-        )
-
-    mine = pl.ds(first, ROWS)
-    partner = 2 * x + 1 - core
-
-    def rows_of(h):
-        return pl.ds(pl.multiple_of(h * ROWS, L), ROWS)
-
-    def share(buf, ss, rs, n):
-        to = partner if n == 0 else 2 * lax.rem(x + n, NX) + core
-        return remote(buf.at[mine], buf.at[mine], ss.at[n], rs.at[n], cell, to)
-
-    def pass_on(buf, ss, rs, n):
-        part = buf.at[rows_of(2 * lax.rem(x - n + NX, NX) + core)]
-        return remote(part, part, ss.at[n], rs.at[n], cell, partner)
-
-    for n in (0, 1, 3, 2):
-        share(b1r, s_b, r_b, n).start()
-    send_a = [
-        remote(ablk.at[peer(r)], abuf.at[mine], s_a.at[r], r_a.at[r], cell, peer(r)) for r in range(1, H)
-    ]
-    for c in send_a:
-        c.start()
-
     a_row = me * SH + lax.broadcasted_iota(jnp.int32, (SH, PB), 0)
 
     def widen_cut(n, carry):
@@ -220,6 +233,12 @@
 
     lax.fori_loop(0, 64, widen_cut, 0, unroll=4)
 
+    for n in (2, 1, 3, 0):
+        own = 2 * lax.rem(x + n, NX) + core
+        pltpu.make_async_copy(zq.at[n], zq.at[n], r_zq.at[n]).wait()
+        zs[own] = jnp.minimum(zs[own], zq[n])
+        if n:
+            ship(n).start()
     send_cut = [
         remote(cutf.at[peer(r)], cutr.at[me], s_cut.at[r], r_cut.at[r], cell, peer(r)) for r in range(1, H)
     ]
@@ -274,19 +293,13 @@
         b2r[pl.ds(first + L * k, L), :] = rows
     for n in (1, 3, 2, 0):
         share(b2r, s_c, r_c, n).start()
-    for c in send_cut[4:]:
-        c.start()
-
-    for c in send_a:
-        c.wait()
-
-    def pick(i, carry):
-        a1[pl.ds(i, 1), :] = abuf[pl.ds(sels[0, i], 1), :]
-        return carry
-
-    lax.fori_loop(0, PB, pick, 0, unroll=8)
+
+    got = zs[me]
+    for n in (1, 3, 2):
+        pltpu.make_async_copy(za.at[n - 1], za.at[n - 1], r_a.at[n]).wait()
+        got = jnp.minimum(got, za[n - 1])
     col = first + lanes((PB, PB))
-    a1[...] = jnp.where(col < count, a1[...], BIG)
+    a1[...] = jnp.where(col < count, got, BIG)
 
     def strip(chip, cc):
         return pl.ds(pl.multiple_of((2 * chip + cc) * SH, SH), SH)
@@ -323,6 +336,8 @@
     for n in (1, 3, 2):
         pltpu.make_async_copy(b2r.at[mine], b2r.at[mine], r_c.at[n]).wait()
         pass_on(b2r, s_cf, r_cf, n).start()
+    for c in send_cut[4:]:
+        c.start()
     def contract(expanded, rows, groups):
         def step(k, acc):
             acc = list(acc)
@@ -478,9 +493,11 @@
         if n < NX - 1:
             pltpu.make_async_copy(a2q.at[0], a2q.at[0], s_p.at[n]).wait()
     for n in range(NX):
+        lend(n).wait_send()
         share(b1r, s_b, r_b, n).wait_send()
         share(b2r, s_c, r_c, n).wait_send()
         if n:
+            ship(n).wait_send()
             pass_on(b1r, s_bf, r_bf, n).wait_send()
             pass_on(b2r, s_cf, r_cf, n).wait_send()
     for r in range(-4, 5):
@@ -528,13 +545,14 @@
     out = pl.pallas_call(
         kernel,
         out_shape=jax.ShapeDtypeStruct((SH, NZ * NY * PB), F32),
-        in_specs=[hbm, pl.BlockSpec(memory_space=pltpu.SMEM), hbm, hbm, hbm],
+        in_specs=[hbm, pl.BlockSpec(memory_space=pltpu.SMEM), hbm, hbm],
         out_specs=hbm,
         scratch_shapes=[
             v(ROWS, CAP),
             v(G, ROWS, PB),
-            v(H, ROWS, PB),
-            v(CAP, PB),
+            v(H, PB, PB),
+            v(NX, PB, PB),
+            v(NX - 1, PB, PB),
             v(PB, PB),
             v(CAP, PB),
             v(PB, PB),
@@ -548,21 +566,20 @@
             v(SH, PB),
             pltpu.VMEM((SH, NZ * NY * PB), jnp.bfloat16),
             pltpu.VMEM((1, PB), jnp.int32),
-            pltpu.SMEM((1, PB), jnp.int32),
             pltpu.VMEM((PB, 8 * PB), jnp.bfloat16),
             v(H, 8, SH, PB),
             v(H, 8, SH, PB),
             v(H, 8, PB, PB),
             v(8, PB, PB),
             v(8, H, SH, PB),
-            sem(H), sem(H), sem(NX), sem(NX), sem(NX), sem(NX), sem(NX), sem(NX), sem(NX), sem(NX), sem(NX), sem(NX), sem(NX), sem(NX),
+            sem(NX), sem(NX), sem(NX), sem(NX), sem(NX), sem(NX), sem(NX), sem(NX), sem(NX), sem(NX), sem(NX), sem(NX), sem(NX), sem(NX), sem(NX), sem(NX),
             sem(H), sem(H), sem(9), sem(2 * H), sem(16), sem(2), sem(2 * NY), sem(2 * NY), sem(H), sem(H),
-            pltpu.SemaphoreType.DMA, sem(4),
+            pltpu.SemaphoreType.DMA, sem(3),
         ],
         compiler_params=pltpu.CompilerParams(
             collective_id=0, has_side_effects=True, vmem_limit_bytes=48 * 1024 * 1024
         ),
-    )(hold(weights), counts, hold(select), hold(select), hold(cut_weights))
+    )(hold(weights), counts, hold(select), hold(cut_weights))
     return out[None]
 
 

time: 64.8 us -> 61.6 us (0.951)
  Pallas kernels: 62.7 us -> 60 us
    pallas_call x1, Pallas kernels: 62.7 us -> 60 us  [per_device(): pl.pallas_call(kernel, out_shape=jax.ShapeDtypeStruct((SH, NZ * NY * PB),...]
where the time goes in v4:
time: 61.6 us; the launch traced here: 61.5 us
  Pallas kernels  60 us (97%)
  local copies, waits for them, and re-layouts  0.8 us (1%)
  between operations  0.66 us (1%)
    pallas_call x1, Pallas kernels, per_device(): pl.pallas_call(kernel, out_shape=jax.ShapeDtypeStruct((SH, NZ * NY * PB),...  60 us

profile of v4, /device:TPU:1, one launch (start us, length us, event | category | flops | bytes accessed | tf_op | source)
XLA Modules:
  0.0 61.5 jit_solution(2136121820886964228)
XLA Ops:
  0.7 60.0 %shard_map.46 = f32[16,8192]{1,0:T(8,128)S(1)} custom-call(f32[1,112,896]{2,1,0:T(8,128)} %w_ref.1, s32[1]{0:T(128)S(6)} %copy.6.count_ref, s32[1,128]{1,0:T(1,128)} %selv_ref.1, bf16[1,16,8192]{2,1,0:T(8,128)(2,1)} %cut_ref.1), custom_call_target="tpu_custom_call" | custom-call | tf_op jit(solution)/shard_map/pallas_call | solution.py:545
  60.7 0.8 %copy.7 = f32[1,16,8192]{2,1,0:T(8,128)} copy(f32[1,16,8192]{2,1,0:T(8,128)S(1)} %bitcast.1) | data formatting | bytes 1048576

commit v5 on v4

--- a/solution.py
+++ b/solution.py
@@ -475,13 +475,13 @@
         def _():
             take(b_near, 0)
 
-        @pl.when(((n == 0) & both_near) | ((n == NY) & jnp.logical_not(both_near)))
+        @pl.when(r > 0)
+        def _():
+            pltpu.make_async_copy(ch.at[jj], ch.at[jj], r_y.at[which * NY + r]).wait()
+
+        @pl.when(((n == 0) & both_near) | ((n == NY - 1) & jnp.logical_not(both_near)))
         def _():
             take(1 - b_near, 1)
-
-        @pl.when(r > 0)
-        def _():
-            pltpu.make_async_copy(ch.at[jj], ch.at[jj], r_y.at[which * NY + r]).wait()
 
         parent(jj)
         return carry

time: 61.6 us -> 61.5 us (level)
  no operation moved by 1% of the time
where the time goes in v5:
time: 61.5 us; the launch traced here: 61.4 us
  Pallas kernels  59.9 us (97%)
  local copies, waits for them, and re-layouts  0.8 us (1%)
  between operations  0.66 us (1%)
    pallas_call x1, Pallas kernels, per_device(): pl.pallas_call(kernel, out_shape=jax.ShapeDtypeStruct((SH, NZ * NY * PB),...  59.9 us

profile of v5, /device:TPU:1, one launch (start us, length us, event | category | flops | bytes accessed | tf_op | source)
XLA Modules:
  0.0 61.4 jit_solution(8268748541278469105)
XLA Ops:
  0.7 59.9 %shard_map.46 = f32[16,8192]{1,0:T(8,128)S(1)} custom-call(f32[1,112,896]{2,1,0:T(8,128)} %w_ref.1, s32[1]{0:T(128)S(6)} %copy.6.count_ref, s32[1,128]{1,0:T(1,128)} %selv_ref.1, bf16[1,16,8192]{2,1,0:T(8,128)(2,1)} %cut_ref.1), custom_call_target="tpu_custom_call" | custom-call | tf_op jit(solution)/shard_map/pallas_call | solution.py:545
  60.6 0.8 %copy.7 = f32[1,16,8192]{2,1,0:T(8,128)} copy(f32[1,16,8192]{2,1,0:T(8,128)S(1)} %bitcast.1) | data formatting | bytes 1048576

commit v6 on v5

--- a/solution.py
+++ b/solution.py
@@ -479,7 +479,7 @@
         def _():
             pltpu.make_async_copy(ch.at[jj], ch.at[jj], r_y.at[which * NY + r]).wait()
 
-        @pl.when(((n == 0) & both_near) | ((n == NY - 1) & jnp.logical_not(both_near)))
+        @pl.when(((n == 0) & both_near) | ((n == NY - 2) & jnp.logical_not(both_near)))
         def _():
             take(1 - b_near, 1)
 

time: 61.5 us -> 61.9 us (level)
  no operation moved by 1% of the time
where the time goes in v6:
time: 61.9 us; the launch traced here: 61.8 us
  Pallas kernels  60.3 us (97%)
  local copies, waits for them, and re-layouts  0.8 us (1%)
  between operations  0.66 us (1%)
    pallas_call x1, Pallas kernels, per_device(): pl.pallas_call(kernel, out_shape=jax.ShapeDtypeStruct((SH, NZ * NY * PB),...  60.3 us

profile of v6, /device:TPU:1, one launch (start us, length us, event | category | flops | bytes accessed | tf_op | source)
XLA Modules:
  0.0 61.8 jit_solution(4808045882623023322)
XLA Ops:
  0.7 60.3 %shard_map.46 = f32[16,8192]{1,0:T(8,128)S(1)} custom-call(f32[1,112,896]{2,1,0:T(8,128)} %w_ref.1, s32[1]{0:T(128)S(6)} %copy.6.count_ref, s32[1,128]{1,0:T(1,128)} %selv_ref.1, bf16[1,16,8192]{2,1,0:T(8,128)(2,1)} %cut_ref.1), custom_call_target="tpu_custom_call" | custom-call | tf_op jit(solution)/shard_map/pallas_call | solution.py:545
  61.0 0.8 %copy.7 = f32[1,16,8192]{2,1,0:T(8,128)} copy(f32[1,16,8192]{2,1,0:T(8,128)S(1)} %bitcast.1) | data formatting | bytes 1048576
